TPU v7x, 512 devices: a whole 4x4x16 slice. The times are simulated.
512 devices in a mesh: wide: 32 (over z, core), narrow: 16 (over y, x).
Axes of the slice: x: 4, y: 4, z: 16, core: 2. Of those that a mesh axis runs over, the one named last changes fastest.
Arguments:
- hidden: bfloat16 [2048, 2048], P('wide'), may hold values from -6 to 6
- attn_gain: float32 [2048], replicated, may hold values from 0.1 to 1.9
- expert_gain: float32 [2048], replicated, may hold values from 0.1 to 1.9
- query_weight: bfloat16 [2048, 2048], P('wide', 'narrow'), may hold values from -0.125 to 0.125
- key_weight: bfloat16 [2048, 2048], P('wide', 'narrow'), may hold values from -0.125 to 0.125
- value_weight: bfloat16 [2048, 2048], P('wide', 'narrow'), may hold values from -0.125 to 0.125
- output_weight: bfloat16 [2048, 2048], P('wide', 'narrow'), may hold values from -0.125 to 0.125
- router_weight: bfloat16 [2048, 64], replicated, may hold values from -0.125 to 0.125
- gate_weight: bfloat16 [64, 2048, 1024], P('wide', None, 'narrow'), may hold values from -0.125 to 0.125
- up_weight: bfloat16 [64, 2048, 1024], P('wide', None, 'narrow'), may hold values from -0.125 to 0.125
- down_weight: bfloat16 [64, 1024, 2048], P('wide', 'narrow'), may hold values from -0.1875 to 0.1875
- prefix_keys: bfloat16 [256, 8, 2048], P('wide', None, 'narrow'), may hold values from -6 to 6
- prefix_values: bfloat16 [256, 8, 2048], P('wide', None, 'narrow'), may hold values from -6 to 6
- cache_keys: bfloat16 [32, 1024, 2048], P('wide', None, 'narrow'), may hold values from -256 to 256
- cache_values: bfloat16 [32, 1024, 2048], P('wide', None, 'narrow'), may hold values from -6 to 6
- parents: int32 [32, 64], P('wide'), may hold values from 0 to 62, as said below
- cache_lengths: int32 [32], P('wide'), may hold values from 1 to 960, 15360 in all
- group_ids: int32 [32], replicated, may hold values from 0 to 7
- expert_ids: int32 [2048, 8], P('wide'), may hold values from 0 to 63, all different within a row; in each aligned block of 64 rows (0 to 63, 64 to 127, ...) at most 9 rows name the same one
- accepted: int32 [32], P('wide'), may hold values from 0 to 63
Outputs:
- layer_out: bfloat16 [2048, 2048], P('wide', 'narrow')
- new_keys: bfloat16 [32, 1024, 2048], P('wide', None, 'narrow')
- new_values: bfloat16 [32, 1024, 2048], P('wide', None, 'narrow')
Inputs may be any that keep to these rules, and one draw needn't show every extreme that they name: `parents`: node 0 of each tree is the root and its own parent; node i > 0 has its parent among nodes max(0, i - 4) to i - 1; the parent of node 63 is node 62. `expert_ids`: the 8 experts of a token differ; among the tokens of one index of wide no expert is named more than 9 times, a bound that some block reaches in some of them.
All inputs are finite; a program needn't handle non-finite values. No bound on the sum of `cache_lengths` on one device may be relied on, other than what follows from the above.
Results may differ from a plain program's by a relative error of at most 0.01.
The roundings to bfloat16 on the way count: a program that leaves them out, or rounds other values in their place, can miss the bound.
Values may be sent and summed in bfloat16 or wider, within the bound.
A program may use at most 64 MiB of HBM per device.

v0:
```python
import math
import jax
import jax.numpy as jnp
from jax import lax
from jax.sharding import PartitionSpec as P

HD = 128
E = 64
SINK = 4
WIN = 512
CAP = 9
norm_eps = 1e-06


def rms_scale(rows, row_gain):
    widened = rows.astype(jnp.float32)
    power_mean = jnp.mean(widened * widened, axis=-1, keepdims=True)
    return (widened * lax.rsqrt(power_mean + norm_eps) * row_gain).astype(jnp.bfloat16)


def tree_links(parents):
    tree_size = parents.shape[-1]
    node_ids = jnp.arange(tree_size, dtype=jnp.int32)
    linked = (node_ids[:, None] == node_ids[None, :]) | (parents[..., :, None] == node_ids)
    jumper = parents
    for doubling in range(tree_size.bit_length()):
        hop_table = (jumper[..., :, None] == node_ids).astype(jnp.float32)
        through = jnp.einsum(
            "...ij,...jk->...ik",
            hop_table,
            linked.astype(jnp.float32),
            precision=lax.Precision.HIGHEST,
        )
        linked = linked | (through > 0.5)
        jumper = jnp.take_along_axis(jumper, jumper, axis=-1)
    depths = jnp.sum(linked.astype(jnp.int32), axis=-1) - 1
    return (linked, depths)


def body(
    hidden,
    attn_gain,
    expert_gain,
    query_weight,
    key_weight,
    value_weight,
    output_weight,
    router_weight,
    gate_weight,
    up_weight,
    down_weight,
    prefix_keys,
    prefix_values,
    cache_keys,
    cache_values,
    parents,
    cache_lengths,
    group_ids,
    expert_ids,
    accepted,
):
    tok_count, model_width = hidden.shape
    req_count, tree_size = parents.shape
    cache_size = cache_keys.shape[1]
    local_width = query_weight.shape[1]
    head_size = HD
    head_count = local_width // head_size
    group_count = prefix_keys.shape[1]
    narrow_count = lax.axis_size("narrow")
    wide_count = lax.axis_size("wide")
    slice_width = model_width // narrow_count
    narrow_pos = lax.axis_index("narrow")
    wide_pos = lax.axis_index("wide")
    scale_factor = 1.0 / math.sqrt(head_size)
    normed = rms_scale(hidden, attn_gain)
    own_groups = lax.dynamic_slice_in_dim(group_ids, wide_pos * req_count, req_count)
    gathered = (
        lax.all_gather(query_weight, "wide", axis=0, tiled=True),
        lax.all_gather(key_weight, "wide", axis=0, tiled=True),
        lax.all_gather(value_weight, "wide", axis=0, tiled=True),
        lax.all_gather(output_weight, "wide", axis=0, tiled=True),
        lax.all_gather(prefix_keys, "wide", axis=0, tiled=True),
        lax.all_gather(prefix_values, "wide", axis=0, tiled=True),
    )
    query_full, key_full, value_full, output_full, shared_keys, shared_values = gathered
    prefix_len = shared_keys.shape[0]
    group_keys = jnp.take(
        shared_keys.reshape(prefix_len, group_count, head_count, head_size), own_groups, axis=1
    )
    group_values = jnp.take(
        shared_values.reshape(prefix_len, group_count, head_count, head_size), own_groups, axis=1
    )
    queries = jnp.dot(normed, query_full, preferred_element_type=jnp.float32).astype(jnp.bfloat16)
    keys_new = jnp.dot(normed, key_full, preferred_element_type=jnp.float32).astype(jnp.bfloat16)
    values_new = jnp.dot(normed, value_full, preferred_element_type=jnp.float32).astype(
        jnp.bfloat16
    )
    block_shape = (req_count, tree_size, head_count, head_size)
    query_blocks = queries.reshape(block_shape)
    key_blocks = keys_new.reshape(block_shape)
    value_blocks = values_new.reshape(block_shape)
    own_keys = cache_keys.reshape(req_count, cache_size, head_count, head_size)
    own_values = cache_values.reshape(req_count, cache_size, head_count, head_size)
    slot_ids = jnp.arange(cache_size, dtype=jnp.int32)
    lengths = cache_lengths[:, None]
    cache_mask = (slot_ids < lengths) & ((slot_ids < SINK) | (slot_ids >= lengths - WIN))
    ancestry, depths = tree_links(parents)
    cache_allowed = cache_mask[:, None, None, :]
    tree_allowed = ancestry[:, None, :, :]
    prefix_scores = (
        jnp.einsum("rqhd,prhd->rhqp", query_blocks, group_keys, preferred_element_type=jnp.float32)
        * scale_factor
    )
    cache_scores = (
        jnp.einsum("rqhd,rkhd->rhqk", query_blocks, own_keys, preferred_element_type=jnp.float32)
        * scale_factor
    )
    tree_scores = (
        jnp.einsum("rqhd,rkhd->rhqk", query_blocks, key_blocks, preferred_element_type=jnp.float32)
        * scale_factor
    )
    row_top = jnp.maximum(
        jnp.max(prefix_scores, axis=-1),
        jnp.maximum(
            jnp.max(jnp.where(cache_allowed, cache_scores, -jnp.inf), axis=-1),
            jnp.max(jnp.where(tree_allowed, tree_scores, -jnp.inf), axis=-1),
        ),
    )[..., None]
    prefix_weights = jnp.exp(prefix_scores - row_top)
    cache_weights = jnp.where(cache_allowed, jnp.exp(cache_scores - row_top), 0.0)
    tree_weights = jnp.where(tree_allowed, jnp.exp(tree_scores - row_top), 0.0)
    row_total = (
        jnp.sum(prefix_weights, axis=-1)
        + jnp.sum(cache_weights, axis=-1)
        + jnp.sum(tree_weights, axis=-1)
    )
    weighted = jnp.einsum(
        "rhqp,prhd->rqhd",
        prefix_weights.astype(jnp.bfloat16),
        group_values,
        preferred_element_type=jnp.float32,
    )
    weighted = weighted + jnp.einsum(
        "rhqk,rkhd->rqhd",
        cache_weights.astype(jnp.bfloat16),
        own_values,
        preferred_element_type=jnp.float32,
    )
    weighted = weighted + jnp.einsum(
        "rhqk,rkhd->rqhd",
        tree_weights.astype(jnp.bfloat16),
        value_blocks,
        preferred_element_type=jnp.float32,
    )
    attended = (
        (weighted / jnp.transpose(row_total, (0, 2, 1))[..., None])
        .astype(jnp.bfloat16)
        .reshape(tok_count, local_width)
    )
    partial_value = lax.dot_general(
        attended, output_full, (((1,), (1,)), ((), ())), preferred_element_type=jnp.float32
    )
    summed = lax.psum(partial_value, "narrow")
    mixed = (hidden.astype(jnp.float32) + summed).astype(jnp.bfloat16)
    mixed_part = lax.dynamic_slice_in_dim(mixed, narrow_pos * slice_width, slice_width, 1)
    normed_moe = rms_scale(mixed, expert_gain)
    logits = jnp.dot(normed_moe, router_weight, preferred_element_type=jnp.float32)
    expert_range = jnp.arange(E, dtype=jnp.int32)
    top_count = expert_ids.shape[1]
    matches = expert_ids[:, :, None] == expert_range
    chosen = jnp.sum(jnp.where(matches, logits[:, None, :], 0.0), axis=-1)
    shares = jax.nn.softmax(chosen, axis=-1)
    flat_experts = expert_ids.reshape(-1)
    expert_table = (flat_experts[:, None] == expert_range).astype(jnp.int32)
    earlier = jnp.cumsum(expert_table, axis=0) - expert_table
    slot_ranks = jnp.sum(earlier * expert_table, axis=1)
    targets = flat_experts * CAP + slot_ranks
    repeated = jnp.broadcast_to(
        normed_moe[:, None, :], (tok_count, top_count, model_width)
    ).reshape(tok_count * top_count, model_width)
    exp_local = gate_weight.shape[0]
    send_rows = jnp.zeros((E * CAP, model_width), jnp.bfloat16).at[targets].set(repeated)
    send_rows = send_rows.reshape(wide_count, exp_local, CAP, model_width)
    routed = lax.all_to_all(send_rows, "wide", split_axis=0, concat_axis=0, tiled=True)
    gate_out = jnp.einsum("secd,edf->secf", routed, gate_weight, preferred_element_type=jnp.float32)
    up_out = jnp.einsum("secd,edf->secf", routed, up_weight, preferred_element_type=jnp.float32)
    activated = (jax.nn.silu(gate_out) * up_out).astype(jnp.bfloat16)
    produced = jnp.einsum(
        "secf,efd->secd", activated, down_weight, preferred_element_type=jnp.float32
    ).astype(jnp.bfloat16)
    returned = lax.all_to_all(produced, "wide", split_axis=0, concat_axis=0, tiled=True)
    fetched = returned.reshape(E * CAP, model_width)[targets].reshape(
        tok_count, top_count, model_width
    )
    partial_moe = jnp.sum(shares[:, :, None] * fetched.astype(jnp.float32), axis=1)
    moe_part = lax.psum_scatter(partial_moe, "narrow", scatter_dimension=1, tiled=True)
    layer_out = (mixed_part.astype(jnp.float32) + moe_part).astype(jnp.bfloat16)
    on_path = jnp.take_along_axis(ancestry, accepted[:, None, None], axis=1)[:, 0, :]
    slots = jnp.where(on_path, cache_lengths[:, None] + depths, cache_size)
    request_rows = jnp.broadcast_to(
        jnp.arange(req_count, dtype=jnp.int32)[:, None], (req_count, tree_size)
    )
    new_keys = cache_keys.at[request_rows, slots].set(
        keys_new.reshape(req_count, tree_size, local_width), mode="drop"
    )
    new_values = cache_values.at[request_rows, slots].set(
        values_new.reshape(req_count, tree_size, local_width), mode="drop"
    )
    return (layer_out, new_keys, new_values)


def solution(mesh):
    in_specs = (
        P("wide", None),
        P(),
        P(),
        P("wide", "narrow"),
        P("wide", "narrow"),
        P("wide", "narrow"),
        P("wide", "narrow"),
        P(),
        P("wide", None, "narrow"),
        P("wide", None, "narrow"),
        P("wide", "narrow", None),
        P("wide", None, "narrow"),
        P("wide", None, "narrow"),
        P("wide", None, "narrow"),
        P("wide", None, "narrow"),
        P("wide", None),
        P("wide"),
        P(),
        P("wide", None),
        P("wide"),
    )
    out_specs = (P("wide", "narrow"), P("wide", None, "narrow"), P("wide", None, "narrow"))
    return jax.shard_map(body, mesh=mesh, in_specs=in_specs, out_specs=out_specs, check_vma=False)
```

profile of v0, /device:TPU:2, one launch (start us, length us, event | category | flops | bytes accessed | tf_op | source)
XLA Modules:
  0.0 689.3 jit_solution(3292197298421425880)
XLA Ops:
  7.2 1.0 copy.120
  8.2 1.1 copy.121
  9.9 1.2 dynamic_slice.6
  13.1 0.7 fusion.116
  13.8 1.1 fusion.39
  14.9 1.0 fusion.30
  15.9 1.4 gather_fusion.1
  17.3 0.7 fusion.117
  18.0 0.8 gather_fusion.2
  18.9 0.8 gather_fusion.3
  19.7 0.8 gather_fusion.4
  20.5 0.8 gather_fusion.5
  21.3 0.8 gather_fusion.6
  22.0 0.2 fusion.24
  22.2 0.2 fusion.25
  22.4 0.2 fusion.26
  22.6 0.2 fusion.27
  22.8 0.2 fusion.28
  23.1 37.7 %all_gather.18 = bf16[256,8,128]{2,0,1:T(8,128)(2,1)S(1)} all-gather(bf16[8,8,128]{2,0,1:T(8,128)(2,1)S(1)} %copy.59), channel_id=1, replica_groups=mesh['wide'=32,'narrow'=16] {'wide'}, dimensions={0}, use_global_device_ids=true | all-gather | bytes 540672 | tf_op jit(solution)/shard_map/all_gather | solution.py:83
  60.8 28.5 %all_gather.20 = bf16[256,8,128]{2,0,1:T(8,128)(2,1)S(1)} all-gather(bf16[8,8,128]{2,0,1:T(8,128)(2,1)S(1)} %copy.60), channel_id=1, replica_groups=mesh['wide'=32,'narrow'=16] {'wide'}, dimensions={0}, use_global_device_ids=true | all-gather | bytes 540672 | tf_op jit(solution)/shard_map/all_gather | solution.py:82
  89.3 30.0 %all_gather.19 = bf16[2048,128]{1,0:T(8,128)(2,1)S(1)} all-gather(bf16[64,128]{1,0:T(8,128)(2,1)S(1)} %copy-done.7), channel_id=1, replica_groups=mesh['wide'=32,'narrow'=16] {'wide'}, dimensions={0}, use_global_device_ids=true | all-gather | bytes 540672 | tf_op jit(solution)/shard_map/all_gather | solution.py:78
  119.2 28.5 %all_gather.21 = bf16[2048,128]{1,0:T(8,128)(2,1)S(1)} all-gather(bf16[64,128]{1,0:T(8,128)(2,1)S(1)} %copy-done.8), channel_id=1, replica_groups=mesh['wide'=32,'narrow'=16] {'wide'}, dimensions={0}, use_global_device_ids=true | all-gather | bytes 540672 | tf_op jit(solution)/shard_map/all_gather | solution.py:79
  147.7 0.3 convolution_convert_fusion.3
  148.0 0.3 convolution_convert_fusion.2
  148.5 0.3 select_reduce_fusion.1
  148.8 0.3 fusion.126
  149.0 0.3 select_reduce_fusion.2
  149.4 0.2 fusion.85
  149.5 0.2 fusion.71
  149.7 0.2 fusion.52
  150.0 0.2 convolution_bitcast_fusion
  150.2 29.9 %all_gather.22 = bf16[2048,128]{1,0:T(8,128)(2,1)S(1)} all-gather(bf16[64,128]{1,0:T(8,128)(2,1)S(1)} %copy-done.9), channel_id=1, replica_groups=mesh['wide'=32,'narrow'=16] {'wide'}, dimensions={0}, use_global_device_ids=true | all-gather | bytes 540672 | tf_op jit(solution)/shard_map/all_gather | solution.py:80
  180.1 0.3 convolution_convert_fusion.1
  180.4 28.5 %all_gather.23 = bf16[2048,128]{1,0:T(8,128)(2,1)S(1)} all-gather(bf16[64,128]{1,0:T(8,128)(2,1)S(1)} %copy-done.10), channel_id=1, replica_groups=mesh['wide'=32,'narrow'=16] {'wide'}, dimensions={0}, use_global_device_ids=true | all-gather | bytes 540672 | tf_op jit(solution)/shard_map/all_gather | solution.py:81
  208.9 0.2 convolution_add_fusion.1
  209.1 1.3 fusion.35
  210.9 1.2 reduce-window.6
  212.1 0.2 slice_reduce_fusion
  212.4 0.1 fusion.58
  212.5 110.2 %all-reduce.3.cloned.1.call-done = f32[64,2048]{1,0:T(8,128)} async-done(((f32[64,2048]{1,0:T(8,128)}), f32[64,2048]{1,0:T(8,128)}) %all-reduce.3.cloned.1.call-update) | async-done | bytes 524304 | tf_op jit(solution)/shard_map/psum | solution.py:163
  322.8 1.2 fusion.36
  324.0 0.1 fusion.38
  324.2 0.5 copy-done.5
  324.7 4.5 scatter_custom_fusion
  329.2 2.8 reshape.738
  332.0 4.8 copy.67
  336.9 125.1 %all_to_all.10 = bf16[32,2,9,2048]{3,1,2,0:T(2,128)(2,1)S(1)} all-to-all(bf16[32,2,9,2048]{3,1,2,0:T(2,128)(2,1)S(1)} %copy.67), channel_id=1, replica_groups=mesh['wide'=32,'narrow'=16] {'wide'}, dimensions={0} | all-to-all | bytes 4718592 | tf_op jit(solution)/shard_map/all_to_all | solution.py:184
  462.0 1.6 fusion.9
  463.6 4.1 fusion.1
  467.6 5.5 copy.70
  473.1 4.1 all-to-all-start.1
  477.2 0.3 reduce-scatter.2.cloned.1.call-start
  477.5 1.2 fusion.127
  478.6 0.2 select_reduce_fusion
  479.0 0.2 fusion.84
  479.3 110.6 %all-to-all-done.1 = bf16[32,2,9,2048]{3,1,2,0:T(2,128)(2,1)S(1)} async-done(((bf16[32,2,9,2048]{3,1,2,0:T(2,128)(2,1)}), bf16[32,2,9,2048]{3,1,2,0:T(2,128)(2,1)S(1)}, u32[]{:S(2)}, u32[]{:S(2)}) %all-to-all-start.1) | async-done | bytes 2359328 | tf_op jit(solution)/shard_map/all_to_all | solution.py:191
  589.9 3.3 copy.71
  593.2 3.4 reshape.739
  596.6 3.3 gather_fusion
  599.9 4.2 fusion
  605.0 0.9 scatter_fusion
  606.0 0.9 scatter_fusion.1
  606.9 74.2 %reduce-scatter.2.cloned.1.call-done = f32[64,128]{1,0:T(8,128)} async-done(((f32[64,2048]{1,0:T(8,128)}), f32[64,128]{1,0:T(8,128)}) %reduce-scatter.2.cloned.1.call-update) | async-done | bytes 32784 | tf_op jit(solution)/shard_map/reduce_scatter | solution.py:196
  681.1 1.4 add_convert_fusion
  (72 shorter events, 1.3 us)
Async XLA Ops:
  7.2 456.4 %copy-start = (bf16[2,64,2048]{2,1,0:T(8,128)(2,1)S(1)}, bf16[2,64,2048]{2,1,0:T(8,128)(2,1)}, u32[]{:S(2)}) copy-start(bf16[2,64,2048]{2,1,0:T(8,128)(2,1)} %param.34) | copy-start | bytes 1572868
  7.2 315.6 %all-reduce.3.cloned.1.call-start = ((), (), s32[]{:S(2)}) async-start(), calls=%async_computation.3 | async-start | bytes 1048576 | tf_op jit(solution)/shard_map/psum | solution.py:163
  8.2 140.2 %copy-start.2 = (bf16[1,1024,128]{2,1,0:T(8,128)(2,1)}, bf16[1,1024,128]{2,1,0:T(8,128)(2,1)S(1)}, u32[]{:S(2)}) copy-start(bf16[1,1024,128]{2,1,0:T(8,128)(2,1)S(1)} %copy.120) | copy-start | bytes 786436
  8.2 14.8 %copy-start.12 = (bf16[8,8,128]{2,1,0:T(8,128)(2,1)S(1)}, bf16[8,8,128]{2,1,0:T(8,128)(2,1)}, u32[]{:S(2)}) copy-start(bf16[8,8,128]{2,1,0:T(8,128)(2,1)} %param.35) | copy-start | bytes 49156
  8.2 14.8 %copy-start.13 = (bf16[8,8,128]{2,1,0:T(8,128)(2,1)S(1)}, bf16[8,8,128]{2,1,0:T(8,128)(2,1)}, u32[]{:S(2)}) copy-start(bf16[8,8,128]{2,1,0:T(8,128)(2,1)} %param.36) | copy-start | bytes 49156
  15.9 73.4 %copy-start.7 = (bf16[64,128]{1,0:T(8,128)(2,1)S(1)}, bf16[64,128]{1,0:T(8,128)(2,1)}, u32[]{:S(2)}) copy-start(bf16[64,128]{1,0:T(8,128)(2,1)} %param.27) | copy-start | bytes 49156
  18.0 101.2 %copy-start.8 = (bf16[64,128]{1,0:T(8,128)(2,1)S(1)}, bf16[64,128]{1,0:T(8,128)(2,1)}, u32[]{:S(2)}) copy-start(bf16[64,128]{1,0:T(8,128)(2,1)} %param.28) | copy-start | bytes 49156
  18.8 128.9 %copy-start.6 = (bf16[64,2048]{1,0:T(8,128)(2,1)S(1)}, bf16[64,2048]{1,0:T(8,128)(2,1)}, u32[]{:S(2)}) copy-start(bf16[64,2048]{1,0:T(8,128)(2,1)} %param.24) | copy-start | bytes 786436
  18.8 128.9 %copy-start.16 = (f32[2048]{0:T(1024)S(1)}, f32[2048]{0:T(1024)}, u32[]{:S(2)}) copy-start(f32[2048]{0:T(1024)} %param.25) | copy-start | bytes 24580
  89.3 61.0 %copy-start.9 = (bf16[64,128]{1,0:T(8,128)(2,1)S(1)}, bf16[64,128]{1,0:T(8,128)(2,1)}, u32[]{:S(2)}) copy-start(bf16[64,128]{1,0:T(8,128)(2,1)} %param.29) | copy-start | bytes 49156
  147.7 32.6 %copy-start.10 = (bf16[64,128]{1,0:T(8,128)(2,1)S(1)}, bf16[64,128]{1,0:T(8,128)(2,1)}, u32[]{:S(2)}) copy-start(bf16[64,128]{1,0:T(8,128)(2,1)} %param.30) | copy-start | bytes 49156
  149.3 61.1 %copy-start.11 = (s32[64,8]{0,1:T(8,128)S(1)}, s32[64,8]{0,1:T(8,128)}, u32[]{:S(2)}) copy-start(s32[64,8]{0,1:T(8,128)} %param.42) | copy-start | bytes 6148
  180.4 143.6 %copy-start.14 = (f32[2048]{0:T(1024)S(1)}, f32[2048]{0:T(1024)}, u32[]{:S(2)}) copy-start(f32[2048]{0:T(1024)} %param.26) | copy-start | bytes 24580
  324.0 0.7 copy-start.5
  336.8 125.2 %copy-start.15 = (bf16[2,2048,64]{1,2,0:T(8,128)(2,1)S(1)}, bf16[2,2048,64]{1,2,0:T(8,128)(2,1)}, u32[]{:S(2)}) copy-start(bf16[2,2048,64]{1,2,0:T(8,128)(2,1)} %param.32) | copy-start | bytes 1572868
  473.1 116.7 %all-to-all-start.1 = ((bf16[32,2,9,2048]{3,1,2,0:T(2,128)(2,1)}), bf16[32,2,9,2048]{3,1,2,0:T(2,128)(2,1)S(1)}, u32[]{:S(2)}, u32[]{:S(2)}) async-start(bf16[32,2,9,2048]{3,1,2,0:T(2,128)(2,1)} %copy.70), calls=%async_computation.1 | async-start | bytes 4718592 | tf_op jit(solution)/shard_map/all_to_all | solution.py:191
  477.2 203.9 %reduce-scatter.2.cloned.1.call-start = ((), (), s32[]{:S(2)}) async-start(), calls=%async_computation.4 | async-start | bytes 557056 | tf_op jit(solution)/shard_map/reduce_scatter | solution.py:196
  599.9 5.1 copy-start.3
  606.0 76.5 %copy-start.4 = (bf16[1024,128]{1,0:T(8,128)(2,1)}, bf16[1024,128]{1,0:T(8,128)(2,1)S(1)}, u32[]{:S(2)}) copy-start(bf16[1024,128]{1,0:T(8,128)(2,1)S(1)} %scatter_fusion) | copy-start | bytes 786436
  606.9 75.6 %copy-start.1 = (bf16[1024,128]{1,0:T(8,128)(2,1)}, bf16[1024,128]{1,0:T(8,128)(2,1)S(1)}, u32[]{:S(2)}) copy-start(bf16[1024,128]{1,0:T(8,128)(2,1)S(1)} %scatter_fusion.1) | copy-start | bytes 786436
Sparse Core Ops, SparseCore 0:
  210.5 112.1 all-reduce.2
  604.3 76.7 reduce-scatter.1
where the time goes:
time: 690 us; the launch traced here: 689 us
  blocking collectives  308 us (45%)
  waiting for transfers between devices  295 us (43%)
  local copies, waits for them, and re-layouts  39.5 us (6%)
  between operations  17.8 us (3%)
  other arithmetic  12.3 us (2%)
  matrix products  12.3 us (2%)
    all_to_all x1, blocking collectives, body(): lax.all_to_all(send_rows, 'wide', split_axis=0, concat_axis=0, tiled=True)  125 us
    all_to_all x1, waiting for transfers between devices, body(): lax.all_to_all(produced, 'wide', split_axis=0, concat_axis=0, tiled=True)  111 us
    psum x1, waiting for transfers between devices, body(): summed = lax.psum(partial_value, 'narrow')  110 us
    reduce_scatter x1, waiting for transfers between devices, body(): lax.psum_scatter(partial_moe, 'narrow', scatter_dimension=1, tiled=True)  74.2 us
    all_gather x1, blocking collectives, body(): lax.all_gather(prefix_values, 'wide', axis=0, tiled=True)  37.7 us
    all_gather x1, blocking collectives, body(): lax.all_gather(query_weight, 'wide', axis=0, tiled=True)  30 us
    all_gather x1, blocking collectives, body(): lax.all_gather(value_weight, 'wide', axis=0, tiled=True)  29.9 us
    all_gather x1, blocking collectives, body(): lax.all_gather(output_weight, 'wide', axis=0, tiled=True)  28.5 us
  transfers between devices with their start and end apart: 3, of which 3 were waited for; matrix products, arithmetic and copies ran while one was open for 1% of the time, Pallas kernels for 0%

commit v1 on v0

--- a/solution.py
+++ b/solution.py
@@ -160,7 +160,7 @@
     partial_value = lax.dot_general(
         attended, output_full, (((1,), (1,)), ((), ())), preferred_element_type=jnp.float32
     )
-    summed = lax.psum(partial_value, "narrow")
+    summed = jnp.sum(lax.all_gather(partial_value, "narrow"), axis=0)
     mixed = (hidden.astype(jnp.float32) + summed).astype(jnp.bfloat16)
     mixed_part = lax.dynamic_slice_in_dim(mixed, narrow_pos * slice_width, slice_width, 1)
     normed_moe = rms_scale(mixed, expert_gain)

time: 690 us -> 664 us (0.962)
  waiting for transfers between devices: 295 us -> 266 us
    psum x1 -> x0, waiting for transfers between devices: 110 us -> none  [body(): summed = lax.psum(partial_value, 'narrow')]
    all_gather x0 -> x1, waiting for transfers between devices: none -> 80.8 us  [body(): summed = jnp.sum(lax.all_gather(partial_value, 'narrow'), axis=0)]
where the time goes in v1:
time: 664 us; the launch traced here: 663 us
  blocking collectives  308 us (46%)
  waiting for transfers between devices  266 us (40%)
  local copies, waits for them, and re-layouts  39.5 us (6%)
  between operations  17.8 us (3%)
  other arithmetic  15.2 us (2%)
  matrix products  12.4 us (2%)
    all_to_all x1, blocking collectives, body(): lax.all_to_all(send_rows, 'wide', split_axis=0, concat_axis=0, tiled=True)  125 us
    all_to_all x1, waiting for transfers between devices, body(): lax.all_to_all(produced, 'wide', split_axis=0, concat_axis=0, tiled=True)  111 us
    all_gather x1, waiting for transfers between devices, body(): summed = jnp.sum(lax.all_gather(partial_value, 'narrow'), axis=0)  80.8 us
    reduce_scatter x1, waiting for transfers between devices, body(): lax.psum_scatter(partial_moe, 'narrow', scatter_dimension=1, tiled=True)  74.2 us
    all_gather x1, blocking collectives, body(): lax.all_gather(prefix_values, 'wide', axis=0, tiled=True)  37.7 us
    all_gather x1, blocking collectives, body(): lax.all_gather(query_weight, 'wide', axis=0, tiled=True)  30 us
    all_gather x1, blocking collectives, body(): lax.all_gather(value_weight, 'wide', axis=0, tiled=True)  29.9 us
    all_gather x1, blocking collectives, body(): lax.all_gather(output_weight, 'wide', axis=0, tiled=True)  28.5 us
  transfers between devices with their start and end apart: 3, of which 3 were waited for; matrix products, arithmetic and copies ran while one was open for 1% of the time, Pallas kernels for 0%

profile of v1, /device:TPU:2, one launch (start us, length us, event | category | flops | bytes accessed | tf_op | source)
XLA Modules:
  0.0 662.8 jit_solution(6962529820947650341)
XLA Ops:
  7.2 1.0 copy.119
  8.2 1.1 copy.120
  9.9 1.2 dynamic_slice.6
  13.1 0.7 fusion.116
  13.8 1.1 fusion.39
  14.9 1.0 fusion.30
  15.9 1.4 gather_fusion.1
  17.3 0.7 fusion.117
  18.0 0.8 gather_fusion.2
  18.9 0.8 gather_fusion.3
  19.7 0.8 gather_fusion.4
  20.5 0.8 gather_fusion.5
  21.3 0.8 gather_fusion.6
  22.0 0.2 fusion.24
  22.2 0.2 fusion.25
  22.4 0.2 fusion.26
  22.6 0.2 fusion.27
  22.8 0.2 fusion.28
  23.1 37.7 %all_gather.24 = bf16[256,8,128]{2,0,1:T(8,128)(2,1)S(1)} all-gather(bf16[8,8,128]{2,0,1:T(8,128)(2,1)S(1)} %copy.59), channel_id=1, replica_groups=mesh['wide'=32,'narrow'=16] {'wide'}, dimensions={0}, use_global_device_ids=true | all-gather | bytes 540672 | tf_op jit(solution)/shard_map/all_gather | solution.py:83
  60.8 28.5 %all_gather.26 = bf16[256,8,128]{2,0,1:T(8,128)(2,1)S(1)} all-gather(bf16[8,8,128]{2,0,1:T(8,128)(2,1)S(1)} %copy.60), channel_id=1, replica_groups=mesh['wide'=32,'narrow'=16] {'wide'}, dimensions={0}, use_global_device_ids=true | all-gather | bytes 540672 | tf_op jit(solution)/shard_map/all_gather | solution.py:82
  89.3 30.0 %all_gather.25 = bf16[2048,128]{1,0:T(8,128)(2,1)S(1)} all-gather(bf16[64,128]{1,0:T(8,128)(2,1)S(1)} %copy-done.7), channel_id=1, replica_groups=mesh['wide'=32,'narrow'=16] {'wide'}, dimensions={0}, use_global_device_ids=true | all-gather | bytes 540672 | tf_op jit(solution)/shard_map/all_gather | solution.py:78
  119.2 28.5 %all_gather.27 = bf16[2048,128]{1,0:T(8,128)(2,1)S(1)} all-gather(bf16[64,128]{1,0:T(8,128)(2,1)S(1)} %copy-done.8), channel_id=1, replica_groups=mesh['wide'=32,'narrow'=16] {'wide'}, dimensions={0}, use_global_device_ids=true | all-gather | bytes 540672 | tf_op jit(solution)/shard_map/all_gather | solution.py:79
  147.7 0.3 convolution_convert_fusion.3
  148.0 0.3 convolution_convert_fusion.2
  148.5 0.3 select_reduce_fusion.1
  148.8 0.3 fusion.126
  149.0 0.3 select_reduce_fusion.2
  149.4 0.2 fusion.85
  149.6 0.2 fusion.71
  149.7 0.2 fusion.52
  150.0 0.2 convolution_bitcast_fusion
  150.2 29.9 %all_gather.28 = bf16[2048,128]{1,0:T(8,128)(2,1)S(1)} all-gather(bf16[64,128]{1,0:T(8,128)(2,1)S(1)} %copy-done.9), channel_id=1, replica_groups=mesh['wide'=32,'narrow'=16] {'wide'}, dimensions={0}, use_global_device_ids=true | all-gather | bytes 540672 | tf_op jit(solution)/shard_map/all_gather | solution.py:80
  180.1 0.3 convolution_convert_fusion.1
  180.4 28.5 %all_gather.29 = bf16[2048,128]{1,0:T(8,128)(2,1)S(1)} all-gather(bf16[64,128]{1,0:T(8,128)(2,1)S(1)} %copy-done.10), channel_id=1, replica_groups=mesh['wide'=32,'narrow'=16] {'wide'}, dimensions={0}, use_global_device_ids=true | all-gather | bytes 540672 | tf_op jit(solution)/shard_map/all_gather | solution.py:81
  208.9 0.2 convolution_add_fusion.1
  209.1 1.3 fusion.35
  210.9 1.2 reduce-window.6
  212.1 0.2 slice_reduce_fusion
  212.6 80.8 %all-gather.3.cloned.1.call-done = f32[1024,2048]{1,0:T(8,128)} async-done(((f32[64,2048]{1,0:T(8,128)}), f32[1024,2048]{1,0:T(8,128)}) %all-gather.3.cloned.1.call-update) | async-done | bytes 8388624 | tf_op jit(solution)/shard_map/all_gather | solution.py:163
  293.3 3.9 reduce_sum.105
  297.3 0.2 fusion.36
  297.5 0.1 fusion.38
  297.6 0.5 copy-done.5
  298.2 4.5 scatter_custom_fusion
  302.7 2.8 reshape.738
  305.5 4.8 copy.67
  310.3 125.1 %all_to_all.10 = bf16[32,2,9,2048]{3,1,2,0:T(2,128)(2,1)S(1)} all-to-all(bf16[32,2,9,2048]{3,1,2,0:T(2,128)(2,1)S(1)} %copy.67), channel_id=1, replica_groups=mesh['wide'=32,'narrow'=16] {'wide'}, dimensions={0} | all-to-all | bytes 4718592 | tf_op jit(solution)/shard_map/all_to_all | solution.py:184
  435.5 1.6 fusion.9
  437.0 4.1 fusion.1
  441.1 5.5 copy.70
  446.6 4.1 all-to-all-start.1
  450.7 0.3 reduce-scatter.2.cloned.1.call-start
  450.9 1.2 fusion.127
  452.1 0.2 select_reduce_fusion
  452.5 0.2 fusion.84
  452.8 110.6 %all-to-all-done.1 = bf16[32,2,9,2048]{3,1,2,0:T(2,128)(2,1)S(1)} async-done(((bf16[32,2,9,2048]{3,1,2,0:T(2,128)(2,1)}), bf16[32,2,9,2048]{3,1,2,0:T(2,128)(2,1)S(1)}, u32[]{:S(2)}, u32[]{:S(2)}) %all-to-all-start.1) | async-done | bytes 2359328 | tf_op jit(solution)/shard_map/all_to_all | solution.py:191
  563.3 3.3 copy.71
  566.7 3.4 reshape.739
  570.0 3.3 gather_fusion
  573.4 4.2 fusion
  578.5 0.9 scatter_fusion
  579.4 0.9 scatter_fusion.1
  580.4 74.2 %reduce-scatter.2.cloned.1.call-done = f32[64,128]{1,0:T(8,128)} async-done(((f32[64,2048]{1,0:T(8,128)}), f32[64,128]{1,0:T(8,128)}) %reduce-scatter.2.cloned.1.call-update) | async-done | bytes 32784 | tf_op jit(solution)/shard_map/reduce_scatter | solution.py:196
  654.6 1.4 add_convert_fusion
  (73 shorter events, 1.4 us)
Async XLA Ops:
  7.2 429.9 %copy-start = (bf16[2,64,2048]{2,1,0:T(8,128)(2,1)S(1)}, bf16[2,64,2048]{2,1,0:T(8,128)(2,1)}, u32[]{:S(2)}) copy-start(bf16[2,64,2048]{2,1,0:T(8,128)(2,1)} %param.34) | copy-start | bytes 1572868
  7.2 286.2 %all-gather.3.cloned.1.call-start = ((), (), s32[]{:S(2)}) async-start(), calls=%async_computation.4 | async-start | bytes 8912896 | tf_op jit(solution)/shard_map/all_gather | solution.py:163
  8.2 140.2 %copy-start.2 = (bf16[1,1024,128]{2,1,0:T(8,128)(2,1)}, bf16[1,1024,128]{2,1,0:T(8,128)(2,1)S(1)}, u32[]{:S(2)}) copy-start(bf16[1,1024,128]{2,1,0:T(8,128)(2,1)S(1)} %copy.119) | copy-start | bytes 786436
  8.2 14.8 %copy-start.12 = (bf16[8,8,128]{2,1,0:T(8,128)(2,1)S(1)}, bf16[8,8,128]{2,1,0:T(8,128)(2,1)}, u32[]{:S(2)}) copy-start(bf16[8,8,128]{2,1,0:T(8,128)(2,1)} %param.35) | copy-start | bytes 49156
  8.2 14.8 %copy-start.13 = (bf16[8,8,128]{2,1,0:T(8,128)(2,1)S(1)}, bf16[8,8,128]{2,1,0:T(8,128)(2,1)}, u32[]{:S(2)}) copy-start(bf16[8,8,128]{2,1,0:T(8,128)(2,1)} %param.36) | copy-start | bytes 49156
  15.9 73.4 %copy-start.7 = (bf16[64,128]{1,0:T(8,128)(2,1)S(1)}, bf16[64,128]{1,0:T(8,128)(2,1)}, u32[]{:S(2)}) copy-start(bf16[64,128]{1,0:T(8,128)(2,1)} %param.27) | copy-start | bytes 49156
  18.0 101.2 %copy-start.8 = (bf16[64,128]{1,0:T(8,128)(2,1)S(1)}, bf16[64,128]{1,0:T(8,128)(2,1)}, u32[]{:S(2)}) copy-start(bf16[64,128]{1,0:T(8,128)(2,1)} %param.28) | copy-start | bytes 49156
  18.8 128.9 %copy-start.6 = (bf16[64,2048]{1,0:T(8,128)(2,1)S(1)}, bf16[64,2048]{1,0:T(8,128)(2,1)}, u32[]{:S(2)}) copy-start(bf16[64,2048]{1,0:T(8,128)(2,1)} %param.24) | copy-start | bytes 786436
  18.8 128.9 %copy-start.16 = (f32[2048]{0:T(1024)S(1)}, f32[2048]{0:T(1024)}, u32[]{:S(2)}) copy-start(f32[2048]{0:T(1024)} %param.25) | copy-start | bytes 24580
  89.3 61.0 %copy-start.9 = (bf16[64,128]{1,0:T(8,128)(2,1)S(1)}, bf16[64,128]{1,0:T(8,128)(2,1)}, u32[]{:S(2)}) copy-start(bf16[64,128]{1,0:T(8,128)(2,1)} %param.29) | copy-start | bytes 49156
  147.7 32.6 %copy-start.10 = (bf16[64,128]{1,0:T(8,128)(2,1)S(1)}, bf16[64,128]{1,0:T(8,128)(2,1)}, u32[]{:S(2)}) copy-start(bf16[64,128]{1,0:T(8,128)(2,1)} %param.30) | copy-start | bytes 49156
  149.3 61.1 %copy-start.11 = (s32[64,8]{0,1:T(8,128)S(1)}, s32[64,8]{0,1:T(8,128)}, u32[]{:S(2)}) copy-start(s32[64,8]{0,1:T(8,128)} %param.42) | copy-start | bytes 6148
  293.3 4.1 copy-start.14
  297.5 0.7 copy-start.5
  310.3 125.2 %copy-start.15 = (bf16[2,2048,64]{1,2,0:T(8,128)(2,1)S(1)}, bf16[2,2048,64]{1,2,0:T(8,128)(2,1)}, u32[]{:S(2)}) copy-start(bf16[2,2048,64]{1,2,0:T(8,128)(2,1)} %param.32) | copy-start | bytes 1572868
  446.6 116.8 %all-to-all-start.1 = ((bf16[32,2,9,2048]{3,1,2,0:T(2,128)(2,1)}), bf16[32,2,9,2048]{3,1,2,0:T(2,128)(2,1)S(1)}, u32[]{:S(2)}, u32[]{:S(2)}) async-start(bf16[32,2,9,2048]{3,1,2,0:T(2,128)(2,1)} %copy.70), calls=%async_computation.1 | async-start | bytes 4718592 | tf_op jit(solution)/shard_map/all_to_all | solution.py:191
  450.7 203.9 %reduce-scatter.2.cloned.1.call-start = ((), (), s32[]{:S(2)}) async-start(), calls=%async_computation.3 | async-start | bytes 557056 | tf_op jit(solution)/shard_map/reduce_scatter | solution.py:196
  573.4 5.1 copy-start.3
  579.4 76.5 %copy-start.4 = (bf16[1024,128]{1,0:T(8,128)(2,1)}, bf16[1024,128]{1,0:T(8,128)(2,1)S(1)}, u32[]{:S(2)}) copy-start(bf16[1024,128]{1,0:T(8,128)(2,1)S(1)} %scatter_fusion) | copy-start | bytes 786436
  580.4 75.6 %copy-start.1 = (bf16[1024,128]{1,0:T(8,128)(2,1)}, bf16[1024,128]{1,0:T(8,128)(2,1)S(1)}, u32[]{:S(2)}) copy-start(bf16[1024,128]{1,0:T(8,128)(2,1)S(1)} %scatter_fusion.1) | copy-start | bytes 786436
Sparse Core Ops, SparseCore 0:
  210.6 82.7 all-gather.2
  577.8 76.7 reduce-scatter.1
